TPU v7x, 256 devices: a whole 4x4x8 slice. The times are simulated.
256 devices in a mesh: row: 16 (over x_lo, z), col: 16 (over x_hi, y, core).
Axes of the slice: x: 4 (x_hi: 2, x_lo: 2; x = x_hi * 2 + x_lo), y: 4, z: 8, core: 2. Of those that a mesh axis runs over, the one named last changes fastest.
Arguments:
- tensor: bfloat16 [4096, 2048, 128], P('row', 'col'), may hold values from -96 to 96
- factor_a: float32 [4096, 128], P(('row', 'col')), may hold values from -4.5 to 4.5
- factor_b: float32 [2048, 128], P(('col', 'row')), may hold values from -4.5 to 4.5
- factor_c: float32 [128, 128], replicated, may hold values from -4.5 to 4.5
Outputs:
- new_a: float32 [4096, 128], P(('row', 'col'))
- new_b: float32 [2048, 128], P(('col', 'row'))
- new_c: float32 [128, 128], replicated
All inputs are finite; a program needn't handle non-finite values.
Results may differ from a plain program's by a relative error of at most 0.01.
Values may be sent and summed in bfloat16 or wider, within the bound.
A program may use at most 128 MiB of HBM per device.

v0:
```python
import jax
import jax.numpy as jnp
from jax import lax
from jax.sharding import PartitionSpec as P

STEPS = 2
damping = 0.9
scaling = 0.25
epsilon = 1e-06


def column_squares(values16):
    return jnp.sum(jnp.square(values16.astype(jnp.float32)), axis=0)


def local_terms(block, tile_a, tile_b, c16):
    rows_i, rows_j, depth = block.shape
    rank = tile_a.shape[1]
    pairs = (
        tile_a.astype(jnp.float32)[:, None, :] * tile_b.astype(jnp.float32)[None, :, :]
    ).astype(jnp.bfloat16)
    pairs = pairs.reshape(rows_i * rows_j, rank)
    model = jnp.dot(pairs, c16.T, preferred_element_type=jnp.float32)
    resid = (block.reshape(rows_i * rows_j, depth).astype(jnp.float32) - model).astype(jnp.bfloat16)
    along = jnp.dot(resid, c16, preferred_element_type=jnp.float32).reshape(rows_i, rows_j, rank)
    grad_a = jnp.sum(along * tile_b.astype(jnp.float32)[None, :, :], axis=1)
    grad_b = jnp.sum(along * tile_a.astype(jnp.float32)[:, None, :], axis=0)
    grad_c = lax.dot_general(
        resid, pairs, (((0,), (0,)), ((), ())), preferred_element_type=jnp.float32
    )
    return (grad_a, grad_b, grad_c)


def local(tensor, factor_a, factor_b, factor_c):
    own_a, own_b, third = (factor_a, factor_b, factor_c)
    for step in range(STEPS):
        a_mine16 = own_a.astype(jnp.bfloat16)
        b_mine16 = own_b.astype(jnp.bfloat16)
        tile_a = lax.all_gather(a_mine16, "col", axis=0, tiled=True)
        tile_b = lax.all_gather(b_mine16, "row", axis=0, tiled=True)
        norm_a, norm_b = lax.psum(
            (column_squares(a_mine16), column_squares(b_mine16)), ("row", "col")
        )
        c16 = third.astype(jnp.bfloat16)
        norm_c = column_squares(c16)
        step_a = scaling / (norm_b * norm_c + epsilon)
        step_b = scaling / (norm_a * norm_c + epsilon)
        step_c = scaling / (norm_a * norm_b + epsilon)
        grad_a, grad_b, grad_c = local_terms(tensor, tile_a, tile_b, c16)
        grad_a = lax.psum_scatter(
            grad_a.astype(jnp.bfloat16), "col", scatter_dimension=0, tiled=True
        ).astype(jnp.float32)
        grad_b = lax.psum_scatter(
            grad_b.astype(jnp.bfloat16), "row", scatter_dimension=0, tiled=True
        ).astype(jnp.float32)
        own_a = damping * own_a + step_a * grad_a
        own_b = damping * own_b + step_b * grad_b
        grad_c = lax.psum(grad_c, ("row", "col"))
        third = damping * third + step_c * grad_c
    return (own_a, own_b, third)


def solution(mesh):
    return jax.shard_map(
        local,
        mesh=mesh,
        in_specs=(P("row", "col", None), P(("row", "col"), None), P(("col", "row"), None), P()),
        out_specs=(P(("row", "col"), None), P(("col", "row"), None), P()),
        check_vma=False,
    )
```

profile of v0, /device:TPU:1, one launch (start us, length us, event | category | flops | bytes accessed | tf_op | source)
XLA Modules:
  0.0 663.4 jit_solution(11993279583761159699)
XLA Ops:
  8.1 0.7 multiply_reduce_fusion.9
  8.8 0.7 multiply_reduce_fusion.7
  9.5 30.3 %all_gather.13 = bf16[128,128]{1,0:T(8,128)(2,1)S(1)} all-gather(bf16[8,128]{1,0:T(8,128)(2,1)S(1)} %get-tuple-element.14), channel_id=1, replica_groups=mesh['row'=16,'col'=16] {'row'}, dimensions={0}, use_global_device_ids=true | all-gather | bytes 34816 | tf_op jit(solution)/shard_map/all_gather | solution.py:40
  39.8 31.7 %all_gather.12 = bf16[256,128]{1,0:T(8,128)(2,1)S(1)} all-gather(bf16[16,128]{1,0:T(8,128)(2,1)S(1)} %get-tuple-element.16), channel_id=1, replica_groups=mesh['row'=16,'col'=16] {'col'}, dimensions={0}, use_global_device_ids=true | all-gather | bytes 69632 | tf_op jit(solution)/shard_map/all_gather | solution.py:39
  71.5 5.6 multiply_convert_fusion.1
  77.1 8.1 %fusion.1 = bf16[32768,128]{1,0:T(8,128)(2,1)S(1)} fusion(bf16[32768,128]{1,0:T(8,128)(2,1)} %bitcast.21, bf16[32768,128]{1,0:T(8,128)(2,1)} %bitcast.25, f32[128,128]{1,0:T(8,128)S(1)} %copy-done.2), kind=kOutput, calls=%fused_computation.3 | convolution fusion | flops 1086341120 | bytes 25231360 | tf_op jit(solution)/shard_map/dot_general | solution.py:23
  85.2 3.2 copy-done
  88.5 6.4 fusion.11
  94.9 0.0 reduce-scatter.3.cloned.1.call-start
  94.9 12.1 %multiply_reduce_fusion.3 = (bf16[256,128]{1,0:T(8,128)(2,1)}, f32[32768,128]{1,0:T(8,128)}) fusion(f32[128,128]{1,0:T(8,128)S(1)} %convert_element_type.111, bf16[32768,128]{1,0:T(8,128)(2,1)} %copy-done, f32[128,128]{1,0:T(8,128)S(1)} %copy-done.2), kind=kOutput, calls=%fused_computation.8 | convolution fusion | flops 1082114048 | bytes 25362432 | tf_op jit(solution)/shard_map/dot_general | solution.py:25
  107.1 7.3 %multiply_reduce_fusion.2 = bf16[128,128]{1,0:T(8,128)(2,1)S(1)} fusion(f32[256,128,128]{2,1,0:T(8,128)} %bitcast.23, f32[256,128]{1,0:T(8,128)S(1)} %convert_element_type.110), kind=kLoop, calls=%fused_computation.7 | loop fusion | flops 8372224 | bytes 16941056 | tf_op jit(solution)/shard_map/reduce_sum | solution.py:27
  114.5 46.3 %all-reduce = bf16[128,128]{1,0:T(8,128)(2,1)S(1)} all-reduce(bf16[128,128]{1,0:T(8,128)(2,1)S(1)} %multiply_reduce_fusion.2), channel_id=3, replica_groups=mesh['row'=16,'col'=16] {'row'}, use_global_device_ids=true, to_apply=%region_8.0.clone | all-reduce | flops 16384 | bytes 65536
  160.8 0.6 dynamic-slice
  162.0 84.4 %all-reduce.3 = (f32[128]{0:T(128)S(1)}, f32[128]{0:T(128)S(1)}) all-reduce(f32[128]{0:T(128)S(1)} %get-tuple-element.15, f32[128]{0:T(128)S(1)} %get-tuple-element.13), channel_id=1, replica_groups=mesh['row'=16,'col'=16] {'row','col'}, use_global_device_ids=true, to_apply=%region_6.0 | all-reduce | flops 256 | bytes 2048 | tf_op jit(solution)/shard_map/psum | solution.py:41
  246.4 81.7 %all-reduce.7.cloned.1.call-done = f32[128,128]{1,0:T(8,128)} async-done(((f32[128,128]{1,0:T(8,128)}), f32[128,128]{1,0:T(8,128)}) %all-reduce.7.cloned.1.call-update) | async-done | bytes 65552 | tf_op jit(solution)/shard_map/psum | solution.py:58
  328.1 0.9 multiply_reduce_fusion.4
  329.1 24.4 %all_gather.15 = bf16[128,128]{1,0:T(8,128)(2,1)S(1)} all-gather(bf16[8,128]{1,0:T(8,128)(2,1)S(1)} %get-tuple-element.12), channel_id=1, replica_groups=mesh['row'=16,'col'=16] {'row'}, dimensions={0}, use_global_device_ids=true | all-gather | bytes 34816 | tf_op jit(solution)/shard_map/all_gather | solution.py:40
  353.5 0.7 multiply_reduce_fusion.6
  354.2 28.8 %all_gather.14 = bf16[256,128]{1,0:T(8,128)(2,1)S(1)} all-gather(bf16[16,128]{1,0:T(8,128)(2,1)S(1)} %get-tuple-element.10), channel_id=1, replica_groups=mesh['row'=16,'col'=16] {'col'}, dimensions={0}, use_global_device_ids=true | all-gather | bytes 69632 | tf_op jit(solution)/shard_map/all_gather | solution.py:39
  383.0 5.6 multiply_convert_fusion
  388.6 8.1 %fusion = bf16[32768,128]{1,0:T(8,128)(2,1)S(1)} fusion(bf16[32768,128]{1,0:T(8,128)(2,1)} %bitcast.19, bf16[128,128]{1,0:T(8,128)(2,1)S(1)} %get-tuple-element.8, bf16[32768,128]{1,0:T(8,128)(2,1)} %bitcast.26), kind=kOutput, calls=%fused_computation.1 | convolution fusion | flops 1086324736 | bytes 25198592 | tf_op jit(solution)/shard_map/dot_general | solution.py:23
  396.8 3.2 copy-done.1
  400.0 6.4 fusion.12
  406.4 12.1 %multiply_reduce_fusion.1 = (bf16[256,128]{1,0:T(8,128)(2,1)}, f32[32768,128]{1,0:T(8,128)}) fusion(f32[128,128]{1,0:T(8,128)S(1)} %convert_element_type.126, bf16[32768,128]{1,0:T(8,128)(2,1)} %copy-done.1, bf16[128,128]{1,0:T(8,128)(2,1)S(1)} %get-tuple-element.8), kind=kOutput, calls=%fused_computation.5 | convolution fusion | flops 1082097664 | bytes 25329664 | tf_op jit(solution)/shard_map/dot_general | solution.py:25
  418.4 0.0 reduce-scatter.5.cloned.1.call-start
  418.5 7.3 %multiply_reduce_fusion = bf16[128,128]{1,0:T(8,128)(2,1)S(1)} fusion(f32[256,128,128]{2,1,0:T(8,128)} %bitcast.24, f32[256,128]{1,0:T(8,128)S(1)} %convert_element_type.125), kind=kLoop, calls=%fused_computation.4 | loop fusion | flops 8372224 | bytes 16941056 | tf_op jit(solution)/shard_map/reduce_sum | solution.py:27
  425.8 47.7 %all-reduce.1 = bf16[128,128]{1,0:T(8,128)(2,1)S(1)} all-reduce(bf16[128,128]{1,0:T(8,128)(2,1)S(1)} %multiply_reduce_fusion), channel_id=5, replica_groups=mesh['row'=16,'col'=16] {'row'}, use_global_device_ids=true, to_apply=%region_18.0.clone | all-reduce | flops 16384 | bytes 65536
  473.5 86.2 %all-reduce.2 = (f32[128]{0:T(128)S(1)}, f32[128]{0:T(128)S(1)}) all-reduce(f32[128]{0:T(128)S(1)} %get-tuple-element.11, f32[128]{0:T(128)S(1)} %get-tuple-element.9), channel_id=1, replica_groups=mesh['row'=16,'col'=16] {'row','col'}, use_global_device_ids=true, to_apply=%region_10.0 | all-reduce | flops 256 | bytes 2048 | tf_op jit(solution)/shard_map/psum | solution.py:41
  559.7 0.6 multiply_add_fusion.4
  560.3 92.8 %all-reduce.9.cloned.1.call-done = f32[128,128]{1,0:T(8,128)} async-done(((f32[128,128]{1,0:T(8,128)}), f32[128,128]{1,0:T(8,128)}) %all-reduce.9.cloned.1.call-update) | async-done | bytes 65552 | tf_op jit(solution)/shard_map/psum | solution.py:58
  653.2 1.5 multiply_add_fusion
  654.6 1.3 multiply_add_fusion.2
  (30 shorter events, 0.3 us)
Async XLA Ops:
  8.0 69.1 %copy-start.2 = (f32[128,128]{1,0:T(8,128)S(1)}, f32[128,128]{1,0:T(8,128)}, u32[]{:S(2)}) copy-start(f32[128,128]{1,0:T(8,128)} %param.7) | copy-start | bytes 196612
  8.0 320.1 %all-reduce.7.cloned.1.call-start = ((), (), s32[]{:S(2)}) async-start(), calls=%async_computation.3 | async-start | bytes 131072 | tf_op jit(solution)/shard_map/psum | solution.py:58
  85.2 3.2 copy-start
  94.9 258.6 %reduce-scatter.3.cloned.1.call-start = ((), (), s32[]{:S(2)}) async-start(), calls=%async_computation.2 | async-start | bytes 69632 | tf_op jit(solution)/shard_map/reduce_scatter | solution.py:50
  107.0 546.1 %all-reduce.9.cloned.1.call-start = ((), (), s32[]{:S(2)}) async-start(), calls=%async_computation.5 | async-start | bytes 131072 | tf_op jit(solution)/shard_map/psum | solution.py:58
  107.1 53.7 %copy-start.7 = (u32[256]{0:T(256)S(1)}, u32[256]{0:T(256)}, u32[]{:S(2)}) copy-start(u32[256]{0:T(256)} %constant.14) | copy-start | bytes 3076
  107.1 221.9 %copy-start.5 = (f32[8,128]{1,0:T(8,128)S(1)}, f32[8,128]{1,0:T(8,128)}, u32[]{:S(2)}) copy-start(f32[8,128]{1,0:T(8,128)} %param.6) | copy-start | bytes 12292
  107.1 246.4 %copy-start.4 = (f32[16,128]{1,0:T(8,128)S(1)}, f32[16,128]{1,0:T(8,128)}, u32[]{:S(2)}) copy-start(f32[16,128]{1,0:T(8,128)} %param.5) | copy-start | bytes 24580
  396.7 3.2 copy-start.1
  418.4 236.2 %reduce-scatter.5.cloned.1.call-start = ((), (), s32[]{:S(2)}) async-start(), calls=%async_computation.4 | async-start | bytes 69632 | tf_op jit(solution)/shard_map/reduce_scatter | solution.py:50
  418.5 234.7 %copy-start.3 = (f32[128,128]{1,0:T(8,128)S(1)}, f32[128,128]{1,0:T(8,128)}, u32[]{:S(2)}) copy-start(f32[128,128]{1,0:T(8,128)} %all-reduce.7.cloned.1.call-done) | copy-start | bytes 196612
  418.5 236.1 %copy-start.6 = (bf16[16,128]{1,0:T(8,128)(2,1)S(1)}, bf16[16,128]{1,0:T(8,128)(2,1)}, u32[]{:S(2)}) copy-start(bf16[16,128]{1,0:T(8,128)(2,1)} %reduce-scatter.3.cloned.1.call-done) | copy-start | bytes 12292
Sparse Core Ops, SparseCore 0:
  95.0 233.1 all-reduce.6
  418.6 234.5 all-reduce.8
Sparse Core Ops, SparseCore 1:
  107.1 58.3 reduce-scatter.2
  560.4 60.9 reduce-scatter.4
where the time goes:
time: 664 us; the launch traced here: 663 us
  blocking collectives  380 us (57%)
  waiting for transfers between devices  175 us (26%)
  matrix products  53.2 us (8%)
  other arithmetic  32.4 us (5%)
  between operations  16.3 us (2%)
  local copies, waits for them, and re-layouts  7.04 us (1%)
    psum x2, waiting for transfers between devices, local(): grad_c = lax.psum(grad_c, ('row', 'col'))  175 us
    psum x2, blocking collectives, local(): lax.psum((column_squares(a_mine16), column_squares(b_mine16)), ('row', 'c...  171 us
    unnamed x2, blocking collectives  94 us
    all_gather x2, blocking collectives, local(): tile_a = lax.all_gather(a_mine16, 'col', axis=0, tiled=True)  60.5 us
    all_gather x2, blocking collectives, local(): tile_b = lax.all_gather(b_mine16, 'row', axis=0, tiled=True)  54.7 us
    dot_general x2, matrix products, local_terms(): jnp.dot(resid, c16, preferred_element_type=jnp.float32)  24.1 us
    dot_general x2, matrix products, local_terms(): model = jnp.dot(pairs, c16.T, preferred_element_type=jnp.float32)  16.2 us
    reduce_sum x2, other arithmetic, local_terms(): grad_b = jnp.sum(along * tile_a.astype(jnp.float32)[:, None, :], axis=0)  14.7 us
  transfers between devices with their start and end apart: 4, of which 2 were waited for; matrix products, arithmetic and copies ran while one was open for 5% of the time, Pallas kernels for 0%

commit v1 on v0

--- a/solution.py
+++ b/solution.py
@@ -55,7 +55,7 @@
         ).astype(jnp.float32)
         own_a = damping * own_a + step_a * grad_a
         own_b = damping * own_b + step_b * grad_b
-        grad_c = lax.psum(grad_c, ("row", "col"))
+        grad_c = lax.psum(lax.psum(grad_c, "row"), "col")
         third = damping * third + step_c * grad_c
     return (own_a, own_b, third)
 

time: 664 us -> 836 us (1.26)
  waiting for transfers between devices: 175 us -> 344 us
    reduce_scatter x2, waiting for transfers between devices: 0.02 us -> 97.6 us  [local(): lax.psum_scatter(grad_a.astype(jnp.bfloat16), 'col', scatter_dimension=0,...]
    psum x2 -> x4, waiting for transfers between devices: 175 us -> 246 us  [local(): grad_c = lax.psum(lax.psum(grad_c, 'row'), 'col')]
  transfers between devices with their start and end apart: 4 -> 6, of which waited for: 2 -> 4; matrix products, arithmetic and copies ran while one was open for 5% -> 4% of each run, Pallas kernels for 0% -> 0%
where the time goes in v1:
time: 836 us; the launch traced here: 834 us
  blocking collectives  382 us (46%)
  waiting for transfers between devices  344 us (41%)
  matrix products  53.1 us (6%)
  other arithmetic  32.3 us (4%)
  between operations  14.9 us (2%)
    psum x4, waiting for transfers between devices, local(): grad_c = lax.psum(lax.psum(grad_c, 'row'), 'col')  246 us
    psum x2, blocking collectives, local(): lax.psum((column_squares(a_mine16), column_squares(b_mine16)), ('row', 'c...  174 us
    reduce_scatter x2, waiting for transfers between devices, local(): lax.psum_scatter(grad_a.astype(jnp.bfloat16), 'col', scatter_dimension=0,...  97.6 us
    unnamed x2, blocking collectives  97.2 us
    all_gather x2, blocking collectives, local(): tile_a = lax.all_gather(a_mine16, 'col', axis=0, tiled=True)  56.3 us
    all_gather x2, blocking collectives, local(): tile_b = lax.all_gather(b_mine16, 'row', axis=0, tiled=True)  55.2 us
    dot_general x2, matrix products, local_terms(): jnp.dot(resid, c16, preferred_element_type=jnp.float32)  24.1 us
  transfers between devices with their start and end apart: 6, of which 4 were waited for; matrix products, arithmetic and copies ran while one was open for 4% of the time, Pallas kernels for 0%

profile of v1, /device:TPU:1, one launch (start us, length us, event | category | flops | bytes accessed | tf_op | source)
XLA Modules:
  0.0 833.8 jit_solution(12217615155700573292)
XLA Ops:
  7.2 0.7 multiply_reduce_fusion.9
  7.9 0.7 multiply_reduce_fusion.7
  8.6 30.3 %all_gather.13 = bf16[128,128]{1,0:T(8,128)(2,1)S(1)} all-gather(bf16[8,128]{1,0:T(8,128)(2,1)S(1)} %get-tuple-element.14), channel_id=1, replica_groups=mesh['row'=16,'col'=16] {'row'}, dimensions={0}, use_global_device_ids=true | all-gather | bytes 34816 | tf_op jit(solution)/shard_map/all_gather | solution.py:40
  38.9 31.7 %all_gather.12 = bf16[256,128]{1,0:T(8,128)(2,1)S(1)} all-gather(bf16[16,128]{1,0:T(8,128)(2,1)S(1)} %get-tuple-element.16), channel_id=1, replica_groups=mesh['row'=16,'col'=16] {'col'}, dimensions={0}, use_global_device_ids=true | all-gather | bytes 69632 | tf_op jit(solution)/shard_map/all_gather | solution.py:39
  70.7 5.6 multiply_convert_fusion.1
  76.3 8.1 fusion.1
  84.4 3.2 copy-done
  87.6 6.4 fusion.11
  94.1 110.6 %all-reduce.9.cloned.1.call-done = f32[128,128]{1,0:T(8,128)} async-done(((f32[128,128]{1,0:T(8,128)}), f32[128,128]{1,0:T(8,128)}) %all-reduce.9.cloned.1.call-update) | async-done | bytes 65552 | tf_op jit(solution)/shard_map/psum | solution.py:58
  204.7 12.1 %multiply_reduce_fusion.3 = (bf16[256,128]{1,0:T(8,128)(2,1)}, f32[32768,128]{1,0:T(8,128)}) fusion(f32[128,128]{1,0:T(8,128)S(1)} %convert_element_type.111, bf16[32768,128]{1,0:T(8,128)(2,1)} %copy-done, f32[128,128]{1,0:T(8,128)S(1)} %copy-done.2), kind=kOutput, calls=%fused_computation.8 | convolution fusion | flops 1082114048 | bytes 25362432 | tf_op jit(solution)/shard_map/dot_general | solution.py:25
  216.9 7.3 multiply_reduce_fusion.2
  224.2 48.5 %all-reduce = bf16[128,128]{1,0:T(8,128)(2,1)S(1)} all-reduce(bf16[128,128]{1,0:T(8,128)(2,1)S(1)} %multiply_reduce_fusion.2), channel_id=3, replica_groups=mesh['row'=16,'col'=16] {'row'}, use_global_device_ids=true, to_apply=%region_8.0.clone | all-reduce | flops 16384 | bytes 65536
  272.7 0.6 dynamic-slice
  273.9 97.7 %all-reduce.3 = (f32[128]{0:T(128)S(1)}, f32[128]{0:T(128)S(1)}) all-reduce(f32[128]{0:T(128)S(1)} %get-tuple-element.15, f32[128]{0:T(128)S(1)} %get-tuple-element.13), channel_id=1, replica_groups=mesh['row'=16,'col'=16] {'row','col'}, use_global_device_ids=true, to_apply=%region_6.0 | all-reduce | flops 256 | bytes 2048 | tf_op jit(solution)/shard_map/psum | solution.py:41
  371.7 0.9 multiply_reduce_fusion.4
  372.6 25.0 %all_gather.15 = bf16[128,128]{1,0:T(8,128)(2,1)S(1)} all-gather(bf16[8,128]{1,0:T(8,128)(2,1)S(1)} %get-tuple-element.12), channel_id=1, replica_groups=mesh['row'=16,'col'=16] {'row'}, dimensions={0}, use_global_device_ids=true | all-gather | bytes 34816 | tf_op jit(solution)/shard_map/all_gather | solution.py:40
  397.6 23.7 %reduce-scatter.3.cloned.1.call-done = bf16[16,128]{1,0:T(8,128)(2,1)} async-done(((bf16[256,128]{1,0:T(8,128)(2,1)}), bf16[16,128]{1,0:T(8,128)(2,1)}) %reduce-scatter.3.cloned.1.call-update) | async-done | bytes 4112 | tf_op jit(solution)/shard_map/reduce_scatter | solution.py:50
  421.3 0.7 multiply_reduce_fusion.6
  422.0 24.5 %all_gather.14 = bf16[256,128]{1,0:T(8,128)(2,1)S(1)} all-gather(bf16[16,128]{1,0:T(8,128)(2,1)S(1)} %get-tuple-element.10), channel_id=1, replica_groups=mesh['row'=16,'col'=16] {'col'}, dimensions={0}, use_global_device_ids=true | all-gather | bytes 69632 | tf_op jit(solution)/shard_map/all_gather | solution.py:39
  446.6 5.6 multiply_convert_fusion
  452.2 8.1 fusion
  460.3 3.2 copy-done.1
  463.5 6.4 fusion.12
  469.9 12.1 %multiply_reduce_fusion.1 = (bf16[256,128]{1,0:T(8,128)(2,1)}, f32[32768,128]{1,0:T(8,128)}) fusion(f32[128,128]{1,0:T(8,128)S(1)} %convert_element_type.126, bf16[32768,128]{1,0:T(8,128)(2,1)} %copy-done.1, bf16[128,128]{1,0:T(8,128)(2,1)S(1)} %get-tuple-element.8), kind=kOutput, calls=%fused_computation.5 | convolution fusion | flops 1082097664 | bytes 25329664 | tf_op jit(solution)/shard_map/dot_general | solution.py:25
  482.1 7.3 multiply_reduce_fusion
  489.4 76.0 %all-reduce.2 = (f32[128]{0:T(128)S(1)}, f32[128]{0:T(128)S(1)}) all-reduce(f32[128]{0:T(128)S(1)} %get-tuple-element.11, f32[128]{0:T(128)S(1)} %get-tuple-element.9), channel_id=1, replica_groups=mesh['row'=16,'col'=16] {'row','col'}, use_global_device_ids=true, to_apply=%region_10.0 | all-reduce | flops 256 | bytes 2048 | tf_op jit(solution)/shard_map/psum | solution.py:41
  565.4 48.8 %all-reduce.1 = bf16[128,128]{1,0:T(8,128)(2,1)S(1)} all-reduce(bf16[128,128]{1,0:T(8,128)(2,1)S(1)} %multiply_reduce_fusion), channel_id=5, replica_groups=mesh['row'=16,'col'=16] {'row'}, use_global_device_ids=true, to_apply=%region_19.0.clone | all-reduce | flops 16384 | bytes 65536
  614.3 0.6 multiply_add_fusion.4
  614.9 73.9 %reduce-scatter.5.cloned.1.call-done = bf16[16,128]{1,0:T(8,128)(2,1)} async-done(((bf16[256,128]{1,0:T(8,128)(2,1)}), bf16[16,128]{1,0:T(8,128)(2,1)}) %reduce-scatter.5.cloned.1.call-update) | async-done | bytes 4112 | tf_op jit(solution)/shard_map/reduce_scatter | solution.py:50
  688.8 1.3 multiply_add_fusion.2
  690.0 135.4 %all-reduce.15.cloned.1.call-done = f32[128,128]{1,0:T(8,128)} async-done(((f32[128,128]{1,0:T(8,128)}), f32[128,128]{1,0:T(8,128)}) %all-reduce.15.cloned.1.call-update) | async-done | bytes 65552 | tf_op jit(solution)/shard_map/psum | solution.py:58
  825.5 1.5 multiply_add_fusion
  (36 shorter events, 0.5 us)
Async XLA Ops:
  7.2 69.1 %copy-start.2 = (f32[128,128]{1,0:T(8,128)S(1)}, f32[128,128]{1,0:T(8,128)}, u32[]{:S(2)}) copy-start(f32[128,128]{1,0:T(8,128)} %param.7) | copy-start | bytes 196612
  7.2 197.5 %all-reduce.9.cloned.1.call-start = ((), (), s32[]{:S(2)}) async-start(), calls=%async_computation.3 | async-start | bytes 131072 | tf_op jit(solution)/shard_map/psum | solution.py:58
  84.4 3.2 copy-start
  94.0 277.6 %all-reduce.11.cloned.1.call-start = ((), (), s32[]{:S(2)}) async-start(), calls=%async_computation.4 | async-start | bytes 131072 | tf_op jit(solution)/shard_map/psum | solution.py:58
  204.7 216.6 %reduce-scatter.3.cloned.1.call-start = ((), (), s32[]{:S(2)}) async-start(), calls=%async_computation.2 | async-start | bytes 69632 | tf_op jit(solution)/shard_map/reduce_scatter | solution.py:50
  216.8 398.0 %all-reduce.13.cloned.1.call-start = ((), (), s32[]{:S(2)}) async-start(), calls=%async_computation.6 | async-start | bytes 131072 | tf_op jit(solution)/shard_map/psum | solution.py:58
  216.9 55.8 %copy-start.7 = (u32[256]{0:T(256)S(1)}, u32[256]{0:T(256)}, u32[]{:S(2)}) copy-start(u32[256]{0:T(256)} %constant.14) | copy-start | bytes 3076
  216.9 155.7 %copy-start.5 = (f32[8,128]{1,0:T(8,128)S(1)}, f32[8,128]{1,0:T(8,128)}, u32[]{:S(2)}) copy-start(f32[8,128]{1,0:T(8,128)} %param.6) | copy-start | bytes 12292
  216.9 204.4 %copy-start.4 = (f32[16,128]{1,0:T(8,128)S(1)}, f32[16,128]{1,0:T(8,128)}, u32[]{:S(2)}) copy-start(f32[16,128]{1,0:T(8,128)} %param.5) | copy-start | bytes 24580
  460.3 3.2 copy-start.1
  482.0 206.8 %reduce-scatter.5.cloned.1.call-start = ((), (), s32[]{:S(2)}) async-start(), calls=%async_computation.5 | async-start | bytes 69632 | tf_op jit(solution)/shard_map/reduce_scatter | solution.py:50
  482.0 206.7 %copy-start.6 = (bf16[16,128]{1,0:T(8,128)(2,1)S(1)}, bf16[16,128]{1,0:T(8,128)(2,1)}, u32[]{:S(2)}) copy-start(bf16[16,128]{1,0:T(8,128)(2,1)} %reduce-scatter.3.cloned.1.call-done) | copy-start | bytes 12292
  482.1 343.4 %copy-start.3 = (f32[128,128]{1,0:T(8,128)S(1)}, f32[128,128]{1,0:T(8,128)}, u32[]{:S(2)}) copy-start(f32[128,128]{1,0:T(8,128)} %all-reduce.11.cloned.1.call-done) | copy-start | bytes 196612
  614.2 211.3 %all-reduce.15.cloned.1.call-start = ((), (), s32[]{:S(2)}) async-start(), calls=%async_computation.7 | async-start | bytes 131072 | tf_op jit(solution)/shard_map/psum | solution.py:58
Sparse Core Ops, SparseCore 0:
  94.2 110.4 all-reduce.8
  207.3 140.9 all-reduce.10
  352.7 68.5 reduce-scatter.2
  482.1 117.6 all-reduce.12
  614.3 74.3 reduce-scatter.4
  691.2 134.2 all-reduce.14
